TPU v7x, 32 devices: a whole 2x2x4 slice. The times are simulated.
32 devices in a mesh: space: 8 (over z, y), leaf: 4 (over x, core).
Axes of the slice: x: 2, y: 2, z: 4, core: 2. Of those that a mesh axis runs over, the one named last changes fastest.
Arguments:
- charges: bfloat16 [16, 262144], P(None, ('space', 'leaf')), may hold values from -6 to 6
- leaf_basis: bfloat16 [2048, 64, 128], P(('space', 'leaf')), may hold values from -0.5 to 0.5
- transfer_one: bfloat16 [256, 64, 512], P(('space', 'leaf')), may hold values from -0.25 to 0.25
- transfer_two: bfloat16 [32, 64, 512], P(('space', 'leaf')), may hold values from -0.25 to 0.25
- nodes_leaf: bfloat16 [2048, 3, 64], P(('space', 'leaf')), may hold values from 0 to 6
- nodes_one: bfloat16 [256, 3, 64], P(('space', 'leaf')), may hold values from 0 to 6
- nodes_two: bfloat16 [32, 3, 64], P(('space', 'leaf')), may hold values from 0 to 6
- links_leaf: int32 [2048, 96], P(('space', 'leaf')), may hold values from -1 to 2047, as said below
- links_one: int32 [256, 96], P(('space', 'leaf')), may hold values from -1 to 255, as said below
- links_two: int32 [32, 96], P(('space', 'leaf')), may hold values from -1 to 31, as said below
Outputs:
- potentials: bfloat16 [16, 262144], P(None, ('space', 'leaf'))
Inputs may be any that keep to these rules, and one draw needn't show every extreme that they name: `links_leaf`: A live source leaf lies on a device whose space index differs from that of the target leaf's device by at most one; live slots of a row come first. `links_one`: A live source cluster lies on a device whose space index differs from that of the target's device by at most one; live slots of a row come first. `links_two`: live slots of a row come first.
All inputs are finite; a program needn't handle non-finite values.
Results may differ from a plain program's by a relative error of at most 0.007.
Values may be sent and summed in bfloat16 or wider, within the bound.
No kernel may reach another device: no remote copies, remote signals or barrier semaphores. Data moves between devices by JAX's collectives and lax.ppermute only.
A program may use at most 128 MiB of HBM per device.

v0:
```python
import functools

import jax
import jax.numpy as jnp
from jax import lax
from jax.experimental import pallas as pl
from jax.experimental.pallas import tpu as pltpu
from jax.sharding import PartitionSpec as P


LOG2E = 1.4426950408889634
SCALE = 0.75
AMPLITUDE = 0.25
CHUNK = 16
UNROLL = 6
F32 = jnp.float32
BF16 = jnp.bfloat16
NT = (((1,), (1,)), ((), ()))


def dot_nt(a, b):
    return lax.dot_general(a, b, NT, preferred_element_type=F32)


def low_half(shape):
    return lax.broadcasted_iota(jnp.int32, shape, 1) < shape[1] // 2


def wide_nodes(ref, pair, count):
    if ref.shape[0] == count:
        parts = [ref[min(2 * pair + side, count - 1)] for side in range(2)]
    else:
        parts = [ref[:, 2 * pair + side, :] for side in range(2)]
    return jnp.concatenate([part.astype(F32) for part in parts], axis=1)


def split(value):
    high = value.astype(BF16).astype(F32)
    rest = value - high
    middle = rest.astype(BF16).astype(F32)
    return high, middle, rest - middle


def norm_of(nodes):
    square = nodes * nodes
    return (square[0:1] + square[1:2] + square[2:3]) * SCALE


def up_kernel(counts, charges, basis, t_one, t_two, n_leaf, n_one, n_two, pack):
    leaf_dev, one_dev, two_dev = counts
    lanes = 0
    for nodes_ref, count in ((n_leaf, leaf_dev), (n_one, one_dev), (n_two, two_dev)):
        for pair in range((count + 1) // 2):
            nodes = wide_nodes(nodes_ref, pair, count)
            ones = jnp.ones((2, 128), F32)
            rows = jnp.concatenate([nodes, *split(norm_of(nodes)), ones], axis=0)
            pack[0:8, lanes : lanes + 128] = rows.astype(BF16)
            lanes += 128
    half = low_half((16, 128))
    for pair in range(leaf_dev // 2):
        at = pair * 256
        both = jnp.concatenate([charges[:, at : at + 128], charges[:, at + 128 : at + 256]], axis=0)
        coef = dot_nt(both, basis[pair * 128 : pair * 128 + 128, :])
        coef = jnp.where(half, coef[:16], coef[16:])
        pack[8:24, pair * 128 : pair * 128 + 128] = coef.astype(BF16)
    start = leaf_dev * 64
    for pair in range(one_dev // 2):
        at = pair * 1024
        both = jnp.concatenate([pack[8:24, at : at + 512], pack[8:24, at + 512 : at + 1024]], axis=0)
        coef = dot_nt(both, t_one[pair * 128 : pair * 128 + 128, :])
        coef = jnp.where(half, coef[:16], coef[16:])
        pack[8:24, start + pair * 128 : start + pair * 128 + 128] = coef.astype(BF16)
    below, start = start, start + one_dev * 64
    for pair in range((two_dev + 1) // 2):
        parts = []
        for q in range(2 * pair, 2 * pair + 2):
            q = min(q, two_dev - 1)
            children = pack[8:24, below + q * 512 : below + q * 512 + 512]
            parts.append(dot_nt(children, t_two[q * 64 : q * 64 + 64, :]))
        coef = jnp.concatenate(parts, axis=1)
        pack[8:24, start + pair * 128 : start + pair * 128 + 128] = coef.astype(BF16)


def odd_slot(shape):
    return lax.broadcasted_iota(jnp.int32, shape, 1) % 2


def prepare_kernel(counts, n_leaf, n_one, n_two, l_leaf, l_one, l_two, gate, main, top, rows, rows_two):
    del gate
    leaf_dev, one_dev, two_dev = counts
    row = 0
    for nodes_ref, count, out in ((n_leaf, leaf_dev, main), (n_one, one_dev, main), (n_two, two_dev, top)):
        if out is top:
            row = 0
        for pair in range((count + 1) // 2):
            nodes = wide_nodes(nodes_ref, pair, count)
            cross = nodes * (-2.0 * SCALE)
            high = cross.astype(BF16).astype(F32)
            n1, n2, n3 = split(norm_of(nodes))
            one = jnp.ones((3, 128), F32)
            zero = jnp.zeros((3, 128), F32)
            tile = jnp.concatenate([high, one, n1, n2, cross - high, zero, n3, zero[0:1]], axis=0)
            out[row : row + 128, :] = tile.T.astype(BF16)
            row += 128
    slots = l_leaf.shape[1]
    axis_leaf = lax.axis_size("leaf")
    first = (lax.axis_index("space") - 1) * axis_leaf
    leaf_rows, one_rows = 3 * axis_leaf * leaf_dev, 3 * axis_leaf * one_dev
    empty = leaf_rows + one_rows
    total = jnp.zeros((1, 1), jnp.int32)
    start = 0
    for ref, shift in ((l_leaf, -first * leaf_dev), (l_one, leaf_rows - first * one_dev)):
        links = ref[...]
        live = links >= 0
        count = jnp.sum(jnp.where(live, 1.0, 0.0), axis=1, keepdims=True).astype(jnp.int32)
        chunks = jnp.maximum((count + (CHUNK - 1)) // CHUNK, 1)
        total = total + jnp.sum(chunks.astype(F32), axis=0, keepdims=True).astype(jnp.int32)
        end = start + links.shape[0]
        rows[start:end, 0:slots] = jnp.where(live, links + shift, empty) ^ odd_slot(links.shape)
        rows[start:end, slots:] = jnp.broadcast_to(chunks, (links.shape[0], 128 - slots))
        start = end
    rows[start : start + 8, :] = jnp.broadcast_to(total, (8, 128))
    n_top = lax.axis_size("space") * axis_leaf * two_dev
    links = l_two[...]
    flip = odd_slot(links.shape) if two_dev > 1 else 0
    rows_two[:, 0:slots] = jnp.where(links >= 0, links, n_top) ^ flip
    rows_two[:, slots:] = jnp.zeros((two_dev, 128 - slots), jnp.int32)


def matern(square):
    value = jnp.maximum(square, 1e-30)
    r = value * lax.rsqrt(value)
    return (r + 1.0) * jnp.exp2(r * (-LOG2E))


def gather_features(table, links, base, half):
    tiles = []
    for g in range(CHUNK // 2):
        first, second = links[base + 2 * g], links[base + 2 * g + 1]
        tile = jnp.where(half, table[first, 0:8, :], table[second, 0:8, :])
        tiles.append(jnp.concatenate([tile, tile], axis=0))
    return jnp.concatenate(tiles, axis=1)


def gather_coefs(table, links, base, half):
    tiles = []
    for g in range(CHUNK // 2):
        first, second = links[base + 2 * g], links[base + 2 * g + 1]
        tiles.append(jnp.where(half, table[first, 8:24, :], table[second, 8:24, :]))
    return jnp.concatenate(tiles, axis=1)


def put_pair(table, row, tile):
    table[row] = tile
    table[row + 1] = jnp.concatenate([tile[:, 64:], tile[:, :64]], axis=1)


def couple_kernel(counts, sizes, places, targets, slots, links, features, *refs):
    leaf_dev, one_dev, _ = counts
    axis_leaf = lax.axis_size("leaf")
    my_leaf = lax.axis_index("leaf")
    parity = lax.axis_index("space") % 2
    side_of = (jnp.int32(1), 2 - 2 * parity, 2 * parity)
    starts = (0, 3 * axis_leaf * leaf_dev)
    blocks, far = refs[: len(sizes)], refs[len(sizes)]
    table = refs[len(sizes) + 1]
    dbufs = refs[len(sizes) + 2 : len(sizes) + 2 + UNROLL]
    kbufs = refs[len(sizes) + 2 + UNROLL :]
    far[...] = jnp.zeros_like(far)
    for row in range(table.shape[0] - 2, table.shape[0]):
        table[row] = jnp.zeros((24, 128), BF16)
    at = 0
    spread_by = 32 if len(places) <= 12 else 4
    for ref, size in zip(blocks, sizes):
        for index in range(size):
            kind, mask = places[at]
            device = side_of[kind] * axis_leaf + (my_leaf ^ mask)
            for first, count, start in ((0, leaf_dev, starts[0]), (leaf_dev, one_dev, starts[1])):
                base = start + device * count

                def one_pair(pair, carry, ref=ref, index=index, first=first, base=base):
                    lane = pl.multiple_of((first // 2 + pair) * 128, 128)
                    put_pair(table, base + 2 * pair, ref[index, :, pl.ds(lane, 128)])
                    return carry

                lax.fori_loop(0, count // 2, one_pair, 0, unroll=min(spread_by, count // 2))
            at += 1
    half8 = low_half((8, 128))
    half16 = low_half((16, 128))
    last_target = targets - 1

    def step(u, state):
        t0, c0, t1, b1, t2, b2 = state
        d_in, d_out = dbufs[u - 1], dbufs[u]
        k_in, k_out = kbufs[u - 1], kbufs[u]
        tt = jnp.minimum(t0, last_target)
        b0 = tt * 128 + c0 * CHUNK
        row = pl.multiple_of(tt * 64, 64)
        d_out[...] = jnp.dot(
            features[pl.ds(row, 64), :],
            gather_features(table, links, b0, half8),
            preferred_element_type=F32,
        )
        coefs = gather_coefs(table, links, b2, half16)
        far[t2] = far[t2] + dot_nt(coefs, k_in[...].astype(BF16))
        for g in range(CHUNK // 2):
            k_out[:, g * 128 : g * 128 + 128] = matern(d_in[:, g * 128 : g * 128 + 128])
        last = c0 + 1 >= links[tt * 128 + slots]
        next_t = jnp.where(last, jnp.minimum(t0 + 1, targets), t0)
        next_c = jnp.where(last, 0, c0 + 1)
        return next_t, next_c, t0, b0, t1, b1

    def body(_, state):
        for u in range(UNROLL):
            state = step(u, state)
        return state

    zero, none = jnp.int32(0), jnp.int32(targets)
    total = links[targets * 128]
    lax.fori_loop(0, (total + 2 + UNROLL - 1) // UNROLL, body, (zero, zero, none, zero, none, zero))


def down_kernel(counts, places, slots, links, features, blocks, far, basis, t_one, t_two, out, table):
    leaf_dev, _, two_dev = counts
    pairs = (two_dev + 1) // 2
    for row in range(table.shape[0] - 2, table.shape[0]):
        table[row] = jnp.zeros((24, 128), BF16)
    axis_leaf = lax.axis_size("leaf")
    my_space, my_leaf = lax.axis_index("space"), lax.axis_index("leaf")
    for index, (space_mask, leaf_mask) in enumerate(places):
        base = ((my_space ^ space_mask) * axis_leaf + (my_leaf ^ leaf_mask)) * two_dev
        for pair in range(pairs):
            tile = blocks[index, :, pair * 128 : pair * 128 + 128]
            if two_dev > 1:
                put_pair(table, base + 2 * pair, tile)
            else:
                table[base] = tile
    half8 = low_half((8, 128))
    half16 = low_half((16, 128))
    for q in range(two_dev):
        far_two = jnp.zeros((16, 64), F32)
        for c in range(slots // CHUNK):
            base = q * 128 + c * CHUNK
            square = jnp.dot(
                features[q * 64 : q * 64 + 64, :],
                gather_features(table, links, base, half8),
                preferred_element_type=F32,
            )
            far_two += dot_nt(gather_coefs(table, links, base, half16), matern(square).astype(BF16))
        local_two = (far_two * AMPLITUDE).astype(BF16)
        down_one = jnp.dot(local_two, t_two[q * 64 : q * 64 + 64, :], preferred_element_type=F32)
        for i in range(8):
            p = q * 8 + i
            local_one = far[leaf_dev + p] * AMPLITUDE + down_one[:, i * 64 : i * 64 + 64]
            down_leaf = jnp.dot(
                local_one.astype(BF16), t_one[p * 64 : p * 64 + 64, :], preferred_element_type=F32
            )
            for j in range(8):
                t = p * 8 + j
                local_leaf = far[t] * AMPLITUDE + down_leaf[:, j * 64 : j * 64 + 64]
                out[:, t * 128 : t * 128 + 128] = jnp.dot(
                    local_leaf.astype(BF16), basis[t * 64 : t * 64 + 64, :], preferred_element_type=F32
                ).astype(BF16)


VMEM = pl.BlockSpec(memory_space=pltpu.VMEM)
SMEM = pl.BlockSpec(memory_space=pltpu.SMEM)


def padded(shape, dtype):
    rows = -(-shape[-2] // 8) * 8 if len(shape) > 1 else 1
    size = rows * (-(-shape[-1] // 128) * 128) * jnp.dtype(dtype).itemsize
    for extent in shape[:-2]:
        size *= extent
    return size


def call(kernel, name, specs, out, scratch, flops, args):
    moved = sum(a.size * a.dtype.itemsize for a in args)
    held = [a for a, spec in zip(args, specs) if spec is VMEM] + jax.tree.leaves(out)
    held_only = name != "up"
    limit = sum(padded(a.shape, a.dtype) for a in held) + sum(padded(a.shape, a.dtype) for a in scratch)
    return pl.pallas_call(
        kernel,
        out_shape=out,
        in_specs=specs,
        out_specs=jax.tree.map(lambda _: VMEM, out),
        scratch_shapes=scratch,
        cost_estimate=pl.CostEstimate(flops=flops, bytes_accessed=moved, transcendentals=0),
        compiler_params=pltpu.CompilerParams(vmem_limit_bytes=min(limit + 6 * 2**20, 60 * 2**20) if held_only else 60 * 2**20),
    )(*args)


def swap(value, axis, mask):
    count = lax.axis_size(axis)
    return lax.ppermute(value, axis, [(i, i ^ mask) for i in range(count)])


def relay(near):
    count = lax.axis_size("space")
    pairs = []
    for s in range(count):
        if s % 2:
            pairs.append((s, s - 2 if s >= 3 else 0))
        else:
            pairs.append((s, s + 2 if s + 2 < count else count - 1))
    return lax.ppermute(near, "space", pairs)


def spread(group, masks, axis):
    order = [0]
    for mask in masks:
        merged = group[0] if len(group) == 1 else jnp.concatenate(group, axis=0)
        group = group + [swap(merged, axis, mask)]
        order = order + [m ^ mask for m in order]
    return group, order


def powers(count):
    return [1 << b for b in reversed(range(count.bit_length() - 1))]


def local_body(
    charges,
    leaf_basis,
    transfer_one,
    transfer_two,
    nodes_leaf,
    nodes_one,
    nodes_two,
    links_leaf,
    links_one,
    links_two,
):
    width = charges.shape[0]
    leaf_dev, rank, leaf_size = leaf_basis.shape
    one_dev = leaf_dev // 8
    two_dev = one_dev // 8
    counts = (leaf_dev, one_dev, two_dev)
    slots = links_leaf.shape[1]
    n_space, n_leaf = lax.axis_size("space"), lax.axis_size("leaf")
    two_lanes = (two_dev + 1) // 2 * 128
    split_at = (leaf_dev + one_dev) * rank
    lanes = split_at + two_lanes

    basis = leaf_basis.reshape(leaf_dev * rank, leaf_size)
    t_one = transfer_one.reshape(one_dev * rank, 8 * rank)
    t_two = transfer_two.reshape(two_dev * rank, 8 * rank)
    nodes_leaf, nodes_one = jnp.swapaxes(nodes_leaf, 0, 1), jnp.swapaxes(nodes_one, 0, 1)
    pack = call(
        functools.partial(up_kernel, counts),
        "up",
        [VMEM] * 7,
        jax.ShapeDtypeStruct((24, lanes), BF16),
        [],
        2 * leaf_dev * rank * leaf_size * width,
        (charges, basis, t_one, t_two, nodes_leaf, nodes_one, nodes_two),
    )
    targets = leaf_dev + one_dev
    main, top, rows, rows_two = call(
        functools.partial(prepare_kernel, counts),
        "prepare",
        [VMEM] * 6 + [pl.BlockSpec(memory_space=pl.ANY)],
        (
            jax.ShapeDtypeStruct((targets * rank, 16), BF16),
            jax.ShapeDtypeStruct((two_lanes, 16), BF16),
            jax.ShapeDtypeStruct((targets + 8, 128), jnp.int32),
            jax.ShapeDtypeStruct((two_dev, 128), jnp.int32),
        ),
        [],
        2**32,
        (nodes_leaf, nodes_one, nodes_two, links_leaf, links_one, links_two, pack),
    )

    own = pack[None]
    near = swap(own, "space", 1)
    far_side = relay(near)
    own_group, order = spread([own], powers(n_leaf), "leaf")
    near_group, _ = spread([near], powers(n_leaf), "leaf")
    far_group, _ = spread([far_side], powers(n_leaf), "leaf")
    received = own_group + near_group + far_group
    sizes = tuple(a.shape[0] for a in received)
    places = tuple((kind, m) for kind in range(3) for m in order)
    table_rows = 3 * n_leaf * (leaf_dev + one_dev) + 2

    far = call(
        functools.partial(couple_kernel, counts, sizes, places, targets, slots),
        "couple",
        [SMEM, VMEM] + [VMEM] * len(sizes),
        jax.ShapeDtypeStruct((targets + 1, width, rank), F32),
        [pltpu.VMEM((table_rows, 24, 128), BF16)] + [pltpu.VMEM((rank, CHUNK * rank), F32)] * (2 * UNROLL),
        2**34,
        (rows.reshape(-1), main, *received),
    )

    two = jnp.concatenate([a[:, :, split_at:] for a in own_group], axis=0)
    two_group, two_order = [two], [0]
    for mask in powers(n_space):
        two_group = [jnp.concatenate(two_group + [swap(two_group[0], "space", mask)], axis=0)]
        two_order = two_order + [m ^ mask for m in two_order]
    two_places = tuple((sm, lm) for sm in two_order for lm in order)
    n_two = n_space * n_leaf * two_dev
    return call(
        functools.partial(down_kernel, counts, two_places, slots),
        "down",
        [SMEM] + [VMEM] * 6,
        jax.ShapeDtypeStruct((width, leaf_dev * leaf_size), BF16),
        [pltpu.VMEM((n_two + 2, 24, 128), BF16)],
        2**24,
        (rows_two.reshape(-1), top, two_group[0], far, basis, t_one, t_two),
    )


def solution(mesh):
    return jax.shard_map(
        local_body,
        mesh=mesh,
        in_specs=(
            P(None, ("space", "leaf")),
            P(("space", "leaf"), None, None),
            P(("space", "leaf"), None, None),
            P(("space", "leaf"), None, None),
            P(("space", "leaf"), None, None),
            P(("space", "leaf"), None, None),
            P(("space", "leaf"), None, None),
            P(("space", "leaf"), None),
            P(("space", "leaf"), None),
            P(("space", "leaf"), None),
        ),
        out_specs=P(None, ("space", "leaf")),
        check_vma=False,
    )
```

profile of v0, /device:TPU:6, one launch (start us, length us, event | category | flops | bytes accessed | tf_op | source)
XLA Modules:
  0.0 94.8 jit_solution(11129367873501375248)
XLA Ops:
  0.0 3.2 %shard_map.100.gate = bf16[24,4736]{1,0:T(8,128)(2,1)} custom-call(bf16[16,8192]{1,0:T(8,128)(2,1)} %charges.1, bf16[4096,128]{1,0:T(8,128)(2,1)} %bitcast.8, bf16[512,512]{1,0:T(8,128)(2,1)} %bitcast.10, bf16[64,512]{1,0:T(8,128)(2,1)} %bitcast.17, bf16[3,64,64]{2,1,0:T(8,128)(2,1)} %bitcast.19, bf16[3,8,64]{2,1,0:T(8,128)(2,1)} %bitcast.21, ...), custom_call_target="tpu_custom_call" | custom-call | flops 16777216 | bytes 1928576 | tf_op jit(solution)/shard_map/pallas_call | solution.py:283
  3.2 0.5 collective-permute-start.5
  3.7 0.0 collective-permute-start
  3.7 0.7 constant_dynamic-update-slice_fusion.4
  4.5 6.2 %collective-permute-done.5.refs_3_ = bf16[1,24,4736]{2,1,0:T(8,128)(2,1)S(1)} collective-permute-done((bf16[1,24,4736]{2,1,0:T(8,128)(2,1)}, bf16[1,24,4736]{2,1,0:T(8,128)(2,1)S(1)}, u32[]{:S(2)}, u32[]{:S(2)}) %collective-permute-start.5) | collective-permute-done | bytes 227360 | tf_op jit(solution)/shard_map/ppermute | solution.py:296
  10.7 0.5 collective-permute-start.6
  11.2 0.0 collective-permute-done.refs_1_
  11.2 1.0 %pad_maximum_fusion = bf16[2,24,4736]{2,1,0:T(8,128)(2,1)S(1)} fusion(bf16[1,24,4736]{2,1,0:T(8,128)(2,1)S(1)} %collective-permute-done.refs_1_, bf16[1,24,4736]{2,1,0:T(8,128)(2,1)} %bitcast.15), kind=kLoop, calls=%fused_computation | loop fusion | flops 227328 | bytes 909312 | tf_op jit(solution)/shard_map/concatenate | solution.py:313
  12.2 0.0 copy-start.2
  12.3 0.0 copy-start.4
  12.3 0.0 copy-start.5
  12.3 0.0 copy-start.6
  12.3 0.0 copy-start.7
  12.3 0.0 copy-start.8
  12.3 0.0 copy-start.9
  12.3 0.1 collective-permute-start.1
  12.4 1.3 %collective-permute-start.8 = (bf16[1,24,4736]{2,1,0:T(8,128)(2,1)S(1)}, bf16[1,24,4736]{2,1,0:T(8,128)(2,1)S(1)}, u32[]{:S(2)}, u32[]{:S(2)}) collective-permute-start(bf16[1,24,4736]{2,1,0:T(8,128)(2,1)S(1)} %collective-permute-done.5.refs_3_), channel_id=1, source_target_pairs={{0,8},{4,0},{8,16},{12,4},{16,24},{20,12},{24,28},{28,20},{1,9},{5... | collective-permute-start | bytes 681992 | tf_op jit(solution)/shard_map/ppermute | solution.py:307
  13.7 3.5 %collective-permute-done.6.refs_4_ = bf16[1,24,4736]{2,1,0:T(8,128)(2,1)S(1)} collective-permute-done((bf16[1,24,4736]{2,1,0:T(8,128)(2,1)S(1)}, bf16[1,24,4736]{2,1,0:T(8,128)(2,1)S(1)}, u32[]{:S(2)}, u32[]{:S(2)}) %collective-permute-start.6) | collective-permute-done | bytes 227360 | tf_op jit(solution)/shard_map/ppermute | solution.py:296
  17.1 0.1 pad_maximum_fusion.1
  17.2 0.1 collective-permute-start.7
  17.3 3.1 %collective-permute-done.8.refs_6_ = bf16[1,24,4736]{2,1,0:T(8,128)(2,1)S(1)} collective-permute-done((bf16[1,24,4736]{2,1,0:T(8,128)(2,1)S(1)}, bf16[1,24,4736]{2,1,0:T(8,128)(2,1)S(1)}, u32[]{:S(2)}, u32[]{:S(2)}) %collective-permute-start.8) | collective-permute-done | bytes 227360 | tf_op jit(solution)/shard_map/ppermute | solution.py:307
  20.4 1.5 %collective-permute-start.9 = (bf16[1,24,4736]{2,1,0:T(8,128)(2,1)S(1)}, bf16[1,24,4736]{2,1,0:T(8,128)(2,1)S(1)}, u32[]{:S(2)}, u32[]{:S(2)}) collective-permute-start(bf16[1,24,4736]{2,1,0:T(8,128)(2,1)S(1)} %collective-permute-done.8.refs_6_), channel_id=1, source_target_pairs={{0,2},{1,3},{2,0},{3,1},{4,6},{5,7},{6,4},{7,5},{8,10},{9,11},{10,... | collective-permute-start | bytes 681992 | tf_op jit(solution)/shard_map/ppermute | solution.py:296
  21.9 0.0 collective-permute-done.1.refs_2_
  21.9 2.7 %collective-permute-start.2 = (bf16[4,24,128]{2,1,0:T(8,128)(2,1)S(1)}, bf16[4,24,128]{2,1,0:T(8,128)(2,1)S(1)}, u32[]{:S(2)}, u32[]{:S(2)}) collective-permute-start(bf16[4,24,128]{2,1,0:T(8,128)(2,1)S(1)} %pad_maximum_fusion.4), channel_id=1, source_target_pairs={{0,16},{4,20},{8,24},{12,28},{16,0},{20,4},{24,8},{28,12},{1,17},{... | collective-permute-start | bytes 73736 | tf_op jit(solution)/shard_map/ppermute | solution.py:296
  24.5 2.9 %collective-permute-done.9.refs_7_ = bf16[1,24,4736]{2,1,0:T(8,128)(2,1)S(1)} collective-permute-done((bf16[1,24,4736]{2,1,0:T(8,128)(2,1)S(1)}, bf16[1,24,4736]{2,1,0:T(8,128)(2,1)S(1)}, u32[]{:S(2)}, u32[]{:S(2)}) %collective-permute-start.9) | collective-permute-done | bytes 227360 | tf_op jit(solution)/shard_map/ppermute | solution.py:296
  27.4 0.1 pad_maximum_fusion.2
  27.5 0.1 collective-permute-start.10
  27.6 0.0 collective-permute-done.2
  27.6 1.6 %collective-permute-start.3 = (bf16[8,24,128]{2,1,0:T(8,128)(2,1)S(1)}, bf16[8,24,128]{2,1,0:T(8,128)(2,1)S(1)}, u32[]{:S(2)}, u32[]{:S(2)}) collective-permute-start(bf16[8,24,128]{2,1,0:T(8,128)(2,1)S(1)} %pad_maximum_fusion.3), channel_id=1, source_target_pairs={{0,8},{4,12},{8,0},{12,4},{16,24},{20,28},{24,16},{28,20},{1,9},{5... | collective-permute-start | bytes 147464 | tf_op jit(solution)/shard_map/ppermute | solution.py:296
  29.2 2.5 %collective-permute-done.3 = bf16[8,24,128]{2,1,0:T(8,128)(2,1)S(1)} collective-permute-done((bf16[8,24,128]{2,1,0:T(8,128)(2,1)S(1)}, bf16[8,24,128]{2,1,0:T(8,128)(2,1)S(1)}, u32[]{:S(2)}, u32[]{:S(2)}) %collective-permute-start.3) | collective-permute-done | bytes 49184 | tf_op jit(solution)/shard_map/ppermute | solution.py:296
  31.8 1.3 %collective-permute-start.4 = (bf16[16,24,128]{2,1,0:T(8,128)(2,1)S(1)}, bf16[16,24,128]{2,1,0:T(8,128)(2,1)S(1)}, u32[]{:S(2)}, u32[]{:S(2)}) collective-permute-start(bf16[16,24,128]{2,1,0:T(8,128)(2,1)S(1)} %get-tuple-element.22), channel_id=1, source_target_pairs={{0,4},{4,0},{8,12},{12,8},{16,20},{20,16},{24,28},{28,24},{1,5},{5... | collective-permute-start | bytes 294920 | tf_op jit(solution)/shard_map/ppermute | solution.py:296
  33.1 0.0 copy-done.2
  33.1 0.0 copy-done.4
  33.1 0.0 copy-done.5
  33.1 0.0 copy-done.6
  33.1 0.0 copy-done.7
  33.1 0.0 copy-done.8
  33.1 0.0 copy-done.9
  33.1 0.7 shard_map.101
  33.8 2.6 %collective-permute-done.4 = bf16[16,24,128]{2,1,0:T(8,128)(2,1)S(1)} collective-permute-done((bf16[16,24,128]{2,1,0:T(8,128)(2,1)S(1)}, bf16[16,24,128]{2,1,0:T(8,128)(2,1)S(1)}, u32[]{:S(2)}, u32[]{:S(2)}) %collective-permute-start.4) | collective-permute-done | bytes 98336 | tf_op jit(solution)/shard_map/ppermute | solution.py:296
  36.5 0.0 collective-permute-done.7.refs_5_
  36.5 0.0 collective-permute-done.10.refs_8_
  36.5 0.0 copy-start
  36.5 0.0 copy-start.1
  36.6 0.0 copy-start.3
  36.6 54.1 %shard_map.102.far = f32[73,16,64]{2,1,0:T(8,128)S(1)} custom-call(s32[10240]{0:T(1024)S(1)} %bitcast.24, bf16[4608,16]{1,0:T(8,128)(2,1)S(1)} %get-tuple-element.12.features, bf16[1,24,4736]{2,1,0:T(8,128)(2,1)S(1)} %bitcast.16, bf16[1,24,4736]{2,1,0:T(8,128)(2,1)S(1)} %collective-permute-done.refs_1_, ...), custom_call_target="tpu_custom_call" | custom-call | flops 17179869184 | bytes 2916352 | tf_op jit(solution)/shard_map/pallas_call | solution.py:283
  90.7 0.0 copy-done.1
  90.7 4.1 %shard_map.103 = bf16[16,8192]{1,0:T(8,128)(2,1)} custom-call(s32[128]{0:T(128)S(1)} %bitcast.23, bf16[128,16]{1,0:T(8,128)(2,1)S(1)} %get-tuple-element.10.features, bf16[32,24,128]{2,1,0:T(8,128)(2,1)S(1)} %constant_dynamic-update-slice_fusion.5.blocks, f32[73,16,64]{2,1,0:T(8,128)S(1)} %shard_map.102.far, bf16[4096,128]{1,0:T(8,128)(2,1)S(1)} %bitcast.9, ...), custom_call_target="tpu_custom_call" | custom-call | flops 16777216 | bytes 2138624 | tf_op jit(solution)/shard_map/pallas_call | solution.py:283
  (9 shorter events, 0.1 us)
Async XLA Ops:
  3.2 7.5 %collective-permute-start.5 = (bf16[1,24,4736]{2,1,0:T(8,128)(2,1)}, bf16[1,24,4736]{2,1,0:T(8,128)(2,1)S(1)}, u32[]{:S(2)}, u32[]{:S(2)}) collective-permute-start(bf16[1,24,4736]{2,1,0:T(8,128)(2,1)} %bitcast.12), channel_id=1, source_target_pairs={{0,4},{4,0},{8,12},{12,8},{16,20},{20,16},{24,28},{28,24},{1,5},{5... | collective-permute-start | bytes 681992 | tf_op jit(solution)/shard_map/ppermute | solution.py:296
  3.7 7.5 %collective-permute-start = (bf16[1,24,4736]{2,1,0:T(8,128)(2,1)}, bf16[1,24,4736]{2,1,0:T(8,128)(2,1)S(1)}, u32[]{:S(2)}, u32[]{:S(2)}) collective-permute-start(bf16[1,24,4736]{2,1,0:T(8,128)(2,1)} %bitcast.13), channel_id=1, source_target_pairs={{0,2},{1,3},{2,0},{3,1},{4,6},{5,7},{6,4},{7,5},{8,10},{9,11},{10,... | collective-permute-start | bytes 681992 | tf_op jit(solution)/shard_map/ppermute | solution.py:296
  10.7 6.4 %collective-permute-start.6 = (bf16[1,24,4736]{2,1,0:T(8,128)(2,1)S(1)}, bf16[1,24,4736]{2,1,0:T(8,128)(2,1)S(1)}, u32[]{:S(2)}, u32[]{:S(2)}) collective-permute-start(bf16[1,24,4736]{2,1,0:T(8,128)(2,1)S(1)} %collective-permute-done.5.refs_3_), channel_id=1, source_target_pairs={{0,2},{1,3},{2,0},{3,1},{4,6},{5,7},{6,4},{7,5},{8,10},{9,11},{10,... | collective-permute-start | bytes 681992 | tf_op jit(solution)/shard_map/ppermute | solution.py:296
  12.2 20.8 %copy-start.2 = (bf16[24,4736]{1,0:T(8,128)(2,1)S(1)}, bf16[24,4736]{1,0:T(8,128)(2,1)}, u32[]{:S(2)}) copy-start(bf16[24,4736]{1,0:T(8,128)(2,1)} %shard_map.100.gate) | copy-start | bytes 681988
  12.3 20.8 %copy-start.4 = (bf16[64,3,64]{2,0,1:T(8,128)(2,1)S(1)}, bf16[64,3,64]{2,0,1:T(8,128)(2,1)}, u32[]{:S(2)}) copy-start(bf16[64,3,64]{2,0,1:T(8,128)(2,1)} %param.14) | copy-start | bytes 73732
  12.3 20.8 %copy-start.5 = (bf16[8,3,64]{2,0,1:T(8,128)(2,1)S(1)}, bf16[8,3,64]{2,0,1:T(8,128)(2,1)}, u32[]{:S(2)}) copy-start(bf16[8,3,64]{2,0,1:T(8,128)(2,1)} %param.15) | copy-start | bytes 9220
  12.3 20.8 %copy-start.6 = (bf16[1,3,64]{2,1,0:T(4,128)(2,1)S(1)}, bf16[1,3,64]{2,1,0:T(4,128)(2,1)}, u32[]{:S(2)}) copy-start(bf16[1,3,64]{2,1,0:T(4,128)(2,1)} %n_two.3) | copy-start | bytes 1156
  12.3 20.8 %copy-start.7 = (s32[64,96]{1,0:T(8,128)S(1)}, s32[64,96]{1,0:T(8,128)}, u32[]{:S(2)}) copy-start(s32[64,96]{1,0:T(8,128)} %l_leaf.1) | copy-start | bytes 73732
  12.3 20.8 %copy-start.8 = (s32[8,96]{1,0:T(8,128)S(1)}, s32[8,96]{1,0:T(8,128)}, u32[]{:S(2)}) copy-start(s32[8,96]{1,0:T(8,128)} %l_one.1) | copy-start | bytes 9220
  12.3 20.8 %copy-start.9 = (s32[1,96]{1,0:T(1,128)S(1)}, s32[1,96]{1,0:T(1,128)}, u32[]{:S(2)}) copy-start(s32[1,96]{1,0:T(1,128)} %l_two.1) | copy-start | bytes 1156
  12.3 9.5 %collective-permute-start.1 = (bf16[2,24,4736]{2,1,0:T(8,128)(2,1)S(1)}, bf16[2,24,4736]{2,1,0:T(8,128)(2,1)S(1)}, u32[]{:S(2)}, u32[]{:S(2)}) collective-permute-start(bf16[2,24,4736]{2,1,0:T(8,128)(2,1)S(1)} %pad_maximum_fusion), channel_id=1, source_target_pairs={{0,1},{1,0},{2,3},{3,2},{4,5},{5,4},{6,7},{7,6},{8,9},{9,8},{10,11... | collective-permute-start | bytes 1363976 | tf_op jit(solution)/shard_map/ppermute | solution.py:296
  12.4 8.0 %collective-permute-start.8 = (bf16[1,24,4736]{2,1,0:T(8,128)(2,1)S(1)}, bf16[1,24,4736]{2,1,0:T(8,128)(2,1)S(1)}, u32[]{:S(2)}, u32[]{:S(2)}) collective-permute-start(bf16[1,24,4736]{2,1,0:T(8,128)(2,1)S(1)} %collective-permute-done.5.refs_3_), channel_id=1, source_target_pairs={{0,8},{4,0},{8,16},{12,4},{16,24},{20,12},{24,28},{28,20},{1,9},{5... | collective-permute-start | bytes 681992 | tf_op jit(solution)/shard_map/ppermute | solution.py:307
  17.2 19.3 %collective-permute-start.7 = (bf16[2,24,4736]{2,1,0:T(8,128)(2,1)S(1)}, bf16[2,24,4736]{2,1,0:T(8,128)(2,1)S(1)}, u32[]{:S(2)}, u32[]{:S(2)}) collective-permute-start(bf16[2,24,4736]{2,1,0:T(8,128)(2,1)S(1)} %pad_maximum_fusion.1), channel_id=1, source_target_pairs={{0,1},{1,0},{2,3},{3,2},{4,5},{5,4},{6,7},{7,6},{8,9},{9,8},{10,11... | collective-permute-start | bytes 1363976 | tf_op jit(solution)/shard_map/ppermute | solution.py:296
  20.4 7.1 %collective-permute-start.9 = (bf16[1,24,4736]{2,1,0:T(8,128)(2,1)S(1)}, bf16[1,24,4736]{2,1,0:T(8,128)(2,1)S(1)}, u32[]{:S(2)}, u32[]{:S(2)}) collective-permute-start(bf16[1,24,4736]{2,1,0:T(8,128)(2,1)S(1)} %collective-permute-done.8.refs_6_), channel_id=1, source_target_pairs={{0,2},{1,3},{2,0},{3,1},{4,6},{5,7},{6,4},{7,5},{8,10},{9,11},{10,... | collective-permute-start | bytes 681992 | tf_op jit(solution)/shard_map/ppermute | solution.py:296
  21.9 5.7 %collective-permute-start.2 = (bf16[4,24,128]{2,1,0:T(8,128)(2,1)S(1)}, bf16[4,24,128]{2,1,0:T(8,128)(2,1)S(1)}, u32[]{:S(2)}, u32[]{:S(2)}) collective-permute-start(bf16[4,24,128]{2,1,0:T(8,128)(2,1)S(1)} %pad_maximum_fusion.4), channel_id=1, source_target_pairs={{0,16},{4,20},{8,24},{12,28},{16,0},{20,4},{24,8},{28,12},{1,17},{... | collective-permute-start | bytes 73736 | tf_op jit(solution)/shard_map/ppermute | solution.py:296
  27.5 9.0 %collective-permute-start.10 = (bf16[2,24,4736]{2,1,0:T(8,128)(2,1)S(1)}, bf16[2,24,4736]{2,1,0:T(8,128)(2,1)S(1)}, u32[]{:S(2)}, u32[]{:S(2)}) collective-permute-start(bf16[2,24,4736]{2,1,0:T(8,128)(2,1)S(1)} %pad_maximum_fusion.2), channel_id=1, source_target_pairs={{0,1},{1,0},{2,3},{3,2},{4,5},{5,4},{6,7},{7,6},{8,9},{9,8},{10,11... | collective-permute-start | bytes 1363976 | tf_op jit(solution)/shard_map/ppermute | solution.py:296
  27.6 4.2 %collective-permute-start.3 = (bf16[8,24,128]{2,1,0:T(8,128)(2,1)S(1)}, bf16[8,24,128]{2,1,0:T(8,128)(2,1)S(1)}, u32[]{:S(2)}, u32[]{:S(2)}) collective-permute-start(bf16[8,24,128]{2,1,0:T(8,128)(2,1)S(1)} %pad_maximum_fusion.3), channel_id=1, source_target_pairs={{0,8},{4,12},{8,0},{12,4},{16,24},{20,28},{24,16},{28,20},{1,9},{5... | collective-permute-start | bytes 147464 | tf_op jit(solution)/shard_map/ppermute | solution.py:296
  31.8 4.7 %collective-permute-start.4 = (bf16[16,24,128]{2,1,0:T(8,128)(2,1)S(1)}, bf16[16,24,128]{2,1,0:T(8,128)(2,1)S(1)}, u32[]{:S(2)}, u32[]{:S(2)}) collective-permute-start(bf16[16,24,128]{2,1,0:T(8,128)(2,1)S(1)} %get-tuple-element.22), channel_id=1, source_target_pairs={{0,4},{4,0},{8,12},{12,8},{16,20},{20,16},{24,28},{28,24},{1,5},{5... | collective-permute-start | bytes 294920 | tf_op jit(solution)/shard_map/ppermute | solution.py:296
  36.5 54.2 %copy-start = (bf16[64,64,128]{2,1,0:T(8,128)(2,1)S(1)}, bf16[64,64,128]{2,1,0:T(8,128)(2,1)}, u32[]{:S(2)}) copy-start(bf16[64,64,128]{2,1,0:T(8,128)(2,1)} %param.11) | copy-start | bytes 3145732
  36.5 54.2 %copy-start.1 = (bf16[8,64,512]{2,1,0:T(8,128)(2,1)S(1)}, bf16[8,64,512]{2,1,0:T(8,128)(2,1)}, u32[]{:S(2)}) copy-start(bf16[8,64,512]{2,1,0:T(8,128)(2,1)} %param.12) | copy-start | bytes 1572868
  36.6 54.2 %copy-start.3 = (bf16[1,64,512]{2,1,0:T(8,128)(2,1)S(1)}, bf16[1,64,512]{2,1,0:T(8,128)(2,1)}, u32[]{:S(2)}) copy-start(bf16[1,64,512]{2,1,0:T(8,128)(2,1)} %param.13) | copy-start | bytes 196612
where the time goes:
time: 95 us; the launch traced here: 94.8 us
  Pallas kernels  62.1 us (65%)
  waiting for transfers between devices  20.9 us (22%)
  starting transfers between devices  9.6 us (10%)
  other arithmetic  1.11 us (1%)
    pallas_call x4, Pallas kernels, call(): pl.pallas_call(kernel, out_shape=out, in_specs=specs, out_specs=jax.tree....  62.1 us
    ppermute x10, waiting for transfers between devices, swap(): return lax.ppermute(value, axis, [(i, i ^ mask) for i in range(count)])  17.8 us
    ppermute x10, starting transfers between devices, swap(): return lax.ppermute(value, axis, [(i, i ^ mask) for i in range(count)])  8.34 us
    ppermute x1, waiting for transfers between devices, relay(): return lax.ppermute(near, 'space', pairs)  3.08 us
  transfers between devices with their start and end apart: 11, of which 6 were waited for; matrix products, arithmetic and copies ran while one was open for 2% of the time, Pallas kernels for 1%

commit v1 on v0

--- a/solution.py
+++ b/solution.py
@@ -12,7 +12,7 @@
 SCALE = 0.75
 AMPLITUDE = 0.25
 CHUNK = 16
-UNROLL = 6
+UNROLL = 8
 F32 = jnp.float32
 BF16 = jnp.bfloat16
 NT = (((1,), (1,)), ((), ()))
@@ -376,11 +376,18 @@
     near = swap(own, "space", 1)
     far_side = relay(near)
     own_group, order = spread([own], powers(n_leaf), "leaf")
-    near_group, _ = spread([near], powers(n_leaf), "leaf")
-    far_group, _ = spread([far_side], powers(n_leaf), "leaf")
-    received = own_group + near_group + far_group
+    masks = powers(n_leaf)
+    last = masks[-1]
+    near_group, part = spread([near], masks[:-1], "leaf")
+    far_group, _ = spread([far_side], masks[:-1], "leaf")
+    crossed = swap(jnp.concatenate(near_group + [far_side], axis=0), "leaf", last)
+    remaining = far_group[1] if len(far_group) == 2 else jnp.concatenate(far_group[1:], axis=0)
+    rest = swap(remaining, "leaf", last)
+    received = own_group + near_group + [crossed] + far_group + [rest]
     sizes = tuple(a.shape[0] for a in received)
-    places = tuple((kind, m) for kind in range(3) for m in order)
+    places = tuple((0, m) for m in order) + tuple((1, m) for m in part) + tuple((1, m ^ last) for m in part)
+    places += ((2, last),) + tuple((2, m) for m in part) + tuple((2, m ^ last) for m in part[1:])
+
     table_rows = 3 * n_leaf * (leaf_dev + one_dev) + 2
 
     far = call(

time: 95 us -> 92.8 us (0.977)
  starting transfers between devices: 9.6 us -> 7.37 us
  waiting for transfers between devices: 20.9 us -> 22.6 us
  Pallas kernels: 62.1 us -> 60.6 us
    ppermute x1, waiting for transfers between devices: 3.08 us -> 6.08 us  [relay(): return lax.ppermute(near, 'space', pairs)]
    pallas_call x4, Pallas kernels: 62.1 us -> 60.6 us  [call(): pl.pallas_call(kernel, out_shape=out, in_specs=specs, out_specs=jax.tree....]
    ppermute x10, starting transfers between devices: 8.34 us -> 6.81 us  [swap(): return lax.ppermute(value, axis, [(i, i ^ mask) for i in range(count)])]
    ppermute x10, waiting for transfers between devices: 17.8 us -> 16.5 us  [swap(): return lax.ppermute(value, axis, [(i, i ^ mask) for i in range(count)])]
  transfers between devices with their start and end apart: 11 -> 11, of which waited for: 6 -> 5; matrix products, arithmetic and copies ran while one was open for 2% -> 2% of each run, Pallas kernels for 1% -> 1%
where the time goes in v1:
time: 92.8 us; the launch traced here: 92.6 us
  Pallas kernels  60.6 us (65%)
  waiting for transfers between devices  22.6 us (24%)
  starting transfers between devices  7.37 us (8%)
  other arithmetic  1.08 us (1%)
    pallas_call x4, Pallas kernels, call(): pl.pallas_call(kernel, out_shape=out, in_specs=specs, out_specs=jax.tree....  60.6 us
    ppermute x10, waiting for transfers between devices, swap(): return lax.ppermute(value, axis, [(i, i ^ mask) for i in range(count)])  16.5 us
    ppermute x10, starting transfers between devices, swap(): return lax.ppermute(value, axis, [(i, i ^ mask) for i in range(count)])  6.81 us
    ppermute x1, waiting for transfers between devices, relay(): return lax.ppermute(near, 'space', pairs)  6.08 us
  transfers between devices with their start and end apart: 11, of which 5 were waited for; matrix products, arithmetic and copies ran while one was open for 2% of the time, Pallas kernels for 1%

profile of v1, /device:TPU:6, one launch (start us, length us, event | category | flops | bytes accessed | tf_op | source)
XLA Modules:
  0.0 92.6 jit_solution(13459752635448936386)
XLA Ops:
  0.0 3.2 %shard_map.100.gate = bf16[24,4736]{1,0:T(8,128)(2,1)} custom-call(bf16[16,8192]{1,0:T(8,128)(2,1)} %charges.1, bf16[4096,128]{1,0:T(8,128)(2,1)} %bitcast.8, bf16[512,512]{1,0:T(8,128)(2,1)} %bitcast.10, bf16[64,512]{1,0:T(8,128)(2,1)} %bitcast.17, bf16[3,64,64]{2,1,0:T(8,128)(2,1)} %bitcast.19, bf16[3,8,64]{2,1,0:T(8,128)(2,1)} %bitcast.21, ...), custom_call_target="tpu_custom_call" | custom-call | flops 16777216 | bytes 1928576 | tf_op jit(solution)/shard_map/pallas_call | solution.py:283
  3.2 0.0 copy-start.2
  3.2 0.0 copy-start.4
  3.2 0.0 copy-start.6
  3.2 0.0 copy-start.7
  3.2 0.0 copy-start.8
  3.2 0.0 copy-start.9
  3.3 0.6 collective-permute-start
  3.9 0.0 collective-permute-start.5
  3.9 6.9 %collective-permute-done.refs_1_ = bf16[1,24,4736]{2,1,0:T(8,128)(2,1)S(1)} collective-permute-done((bf16[1,24,4736]{2,1,0:T(8,128)(2,1)}, bf16[1,24,4736]{2,1,0:T(8,128)(2,1)S(1)}, u32[]{:S(2)}, u32[]{:S(2)}) %collective-permute-start) | collective-permute-done | bytes 227360 | tf_op jit(solution)/shard_map/ppermute | solution.py:296
  10.8 1.0 %pad_maximum_fusion.1 = bf16[2,24,4736]{2,1,0:T(8,128)(2,1)S(1)} fusion(bf16[1,24,4736]{2,1,0:T(8,128)(2,1)S(1)} %collective-permute-done.refs_1_, bf16[1,24,4736]{2,1,0:T(8,128)(2,1)} %bitcast.14), kind=kLoop, calls=%fused_computation.1 | loop fusion | flops 227328 | bytes 909312 | tf_op jit(solution)/shard_map/concatenate | solution.py:313
  11.8 0.1 collective-permute-start.1
  11.9 0.0 collective-permute-done.5.refs_3_
  11.9 0.6 collective-permute-start.7
  12.5 0.7 constant_dynamic-update-slice_fusion.4
  13.2 0.6 collective-permute-start.6
  13.8 6.1 %collective-permute-done.7.refs_6_ = bf16[1,24,4736]{2,1,0:T(8,128)(2,1)S(1)} collective-permute-done((bf16[1,24,4736]{2,1,0:T(8,128)(2,1)S(1)}, bf16[1,24,4736]{2,1,0:T(8,128)(2,1)S(1)}, u32[]{:S(2)}, u32[]{:S(2)}) %collective-permute-start.7) | collective-permute-done | bytes 227360 | tf_op jit(solution)/shard_map/ppermute | solution.py:307
  19.9 0.5 collective-permute-start.9
  20.4 0.0 collective-permute-done.1.refs_2_
  20.4 2.7 %collective-permute-start.2 = (bf16[4,24,128]{2,1,0:T(8,128)(2,1)S(1)}, bf16[4,24,128]{2,1,0:T(8,128)(2,1)S(1)}, u32[]{:S(2)}, u32[]{:S(2)}) collective-permute-start(bf16[4,24,128]{2,1,0:T(8,128)(2,1)S(1)} %pad_maximum_fusion.3), channel_id=1, source_target_pairs={{0,16},{4,20},{8,24},{12,28},{16,0},{20,4},{24,8},{28,12},{1,17},{... | collective-permute-start | bytes 73736 | tf_op jit(solution)/shard_map/ppermute | solution.py:296
  23.1 0.0 collective-permute-done.6.refs_4_
  23.1 0.1 pad_maximum_fusion
  23.2 0.1 collective-permute-start.8
  23.3 3.7 %collective-permute-done.9.refs_7_ = bf16[1,24,4736]{2,1,0:T(8,128)(2,1)S(1)} collective-permute-done((bf16[1,24,4736]{2,1,0:T(8,128)(2,1)S(1)}, bf16[1,24,4736]{2,1,0:T(8,128)(2,1)S(1)}, u32[]{:S(2)}, u32[]{:S(2)}) %collective-permute-start.9) | collective-permute-done | bytes 227360 | tf_op jit(solution)/shard_map/ppermute | solution.py:296
  26.9 0.0 collective-permute-start.10
  26.9 0.0 collective-permute-done.2
  26.9 1.6 %collective-permute-start.3 = (bf16[8,24,128]{2,1,0:T(8,128)(2,1)S(1)}, bf16[8,24,128]{2,1,0:T(8,128)(2,1)S(1)}, u32[]{:S(2)}, u32[]{:S(2)}) collective-permute-start(bf16[8,24,128]{2,1,0:T(8,128)(2,1)S(1)} %pad_maximum_fusion.2), channel_id=1, source_target_pairs={{0,8},{4,12},{8,0},{12,4},{16,24},{20,28},{24,16},{28,20},{1,9},{5... | collective-permute-start | bytes 147464 | tf_op jit(solution)/shard_map/ppermute | solution.py:296
  28.6 2.6 %collective-permute-done.3 = bf16[8,24,128]{2,1,0:T(8,128)(2,1)S(1)} collective-permute-done((bf16[8,24,128]{2,1,0:T(8,128)(2,1)S(1)}, bf16[8,24,128]{2,1,0:T(8,128)(2,1)S(1)}, u32[]{:S(2)}, u32[]{:S(2)}) %collective-permute-start.3) | collective-permute-done | bytes 49184 | tf_op jit(solution)/shard_map/ppermute | solution.py:296
  31.2 0.6 collective-permute-start.4
  31.8 0.0 copy-done.2
  31.8 0.0 copy-done.4
  31.8 0.0 copy-done.5
  31.8 0.0 copy-done.6
  31.8 0.0 copy-done.7
  31.8 0.0 copy-done.8
  31.8 0.0 copy-done.9
  31.8 0.7 shard_map.101
  32.5 3.3 %collective-permute-done.4 = bf16[16,24,128]{2,1,0:T(8,128)(2,1)S(1)} collective-permute-done((bf16[16,24,128]{2,1,0:T(8,128)(2,1)S(1)}, bf16[16,24,128]{2,1,0:T(8,128)(2,1)S(1)}, u32[]{:S(2)}, u32[]{:S(2)}) %collective-permute-start.4) | collective-permute-done | bytes 98336 | tf_op jit(solution)/shard_map/ppermute | solution.py:296
  35.9 0.0 collective-permute-done.10.refs_8_
  35.9 0.0 collective-permute-done.8.refs_5_
  35.9 0.0 copy-start
  35.9 0.0 copy-start.1
  35.9 0.0 copy-start.3
  35.9 52.6 %shard_map.102.far = f32[73,16,64]{2,1,0:T(8,128)S(1)} custom-call(s32[10240]{0:T(1024)S(1)} %bitcast.24, bf16[4608,16]{1,0:T(8,128)(2,1)S(1)} %get-tuple-element.12.features, bf16[1,24,4736]{2,1,0:T(8,128)(2,1)S(1)} %bitcast.16, bf16[1,24,4736]{2,1,0:T(8,128)(2,1)S(1)} %collective-permute-done.refs_1_, ...), custom_call_target="tpu_custom_call" | custom-call | flops 17179869184 | bytes 2916352 | tf_op jit(solution)/shard_map/pallas_call | solution.py:283
  88.5 0.0 copy-done
  88.5 0.0 copy-done.1
  88.6 0.0 copy-done.3
  88.6 4.1 %shard_map.103 = bf16[16,8192]{1,0:T(8,128)(2,1)} custom-call(s32[128]{0:T(128)S(1)} %bitcast.23, bf16[128,16]{1,0:T(8,128)(2,1)S(1)} %get-tuple-element.10.features, bf16[32,24,128]{2,1,0:T(8,128)(2,1)S(1)} %constant_dynamic-update-slice_fusion.5.blocks, f32[73,16,64]{2,1,0:T(8,128)S(1)} %shard_map.102.far, bf16[4096,128]{1,0:T(8,128)(2,1)S(1)} %bitcast.9, ...), custom_call_target="tpu_custom_call" | custom-call | flops 16777216 | bytes 2138624 | tf_op jit(solution)/shard_map/pallas_call | solution.py:283
  (8 shorter events, 0.1 us)
Async XLA Ops:
  3.2 28.6 %copy-start.2 = (bf16[24,4736]{1,0:T(8,128)(2,1)S(1)}, bf16[24,4736]{1,0:T(8,128)(2,1)}, u32[]{:S(2)}) copy-start(bf16[24,4736]{1,0:T(8,128)(2,1)} %shard_map.100.gate) | copy-start | bytes 681988
  3.2 28.6 %copy-start.4 = (bf16[64,3,64]{2,0,1:T(8,128)(2,1)S(1)}, bf16[64,3,64]{2,0,1:T(8,128)(2,1)}, u32[]{:S(2)}) copy-start(bf16[64,3,64]{2,0,1:T(8,128)(2,1)} %param.14) | copy-start | bytes 73732
  3.2 28.6 %copy-start.5 = (bf16[8,3,64]{2,0,1:T(8,128)(2,1)S(1)}, bf16[8,3,64]{2,0,1:T(8,128)(2,1)}, u32[]{:S(2)}) copy-start(bf16[8,3,64]{2,0,1:T(8,128)(2,1)} %param.15) | copy-start | bytes 9220
  3.2 28.6 %copy-start.6 = (bf16[1,3,64]{2,1,0:T(4,128)(2,1)S(1)}, bf16[1,3,64]{2,1,0:T(4,128)(2,1)}, u32[]{:S(2)}) copy-start(bf16[1,3,64]{2,1,0:T(4,128)(2,1)} %n_two.3) | copy-start | bytes 1156
  3.2 28.5 %copy-start.7 = (s32[64,96]{1,0:T(8,128)S(1)}, s32[64,96]{1,0:T(8,128)}, u32[]{:S(2)}) copy-start(s32[64,96]{1,0:T(8,128)} %l_leaf.1) | copy-start | bytes 73732
  3.2 28.5 %copy-start.8 = (s32[8,96]{1,0:T(8,128)S(1)}, s32[8,96]{1,0:T(8,128)}, u32[]{:S(2)}) copy-start(s32[8,96]{1,0:T(8,128)} %l_one.1) | copy-start | bytes 9220
  3.2 28.5 %copy-start.9 = (s32[1,96]{1,0:T(1,128)S(1)}, s32[1,96]{1,0:T(1,128)}, u32[]{:S(2)}) copy-start(s32[1,96]{1,0:T(1,128)} %l_two.1) | copy-start | bytes 1156
  3.3 7.6 %collective-permute-start = (bf16[1,24,4736]{2,1,0:T(8,128)(2,1)}, bf16[1,24,4736]{2,1,0:T(8,128)(2,1)S(1)}, u32[]{:S(2)}, u32[]{:S(2)}) collective-permute-start(bf16[1,24,4736]{2,1,0:T(8,128)(2,1)} %bitcast.12), channel_id=1, source_target_pairs={{0,2},{1,3},{2,0},{3,1},{4,6},{5,7},{6,4},{7,5},{8,10},{9,11},{10,... | collective-permute-start | bytes 681992 | tf_op jit(solution)/shard_map/ppermute | solution.py:296
  3.9 8.0 %collective-permute-start.5 = (bf16[1,24,4736]{2,1,0:T(8,128)(2,1)}, bf16[1,24,4736]{2,1,0:T(8,128)(2,1)S(1)}, u32[]{:S(2)}, u32[]{:S(2)}) collective-permute-start(bf16[1,24,4736]{2,1,0:T(8,128)(2,1)} %bitcast.13), channel_id=1, source_target_pairs={{0,4},{4,0},{8,12},{12,8},{16,20},{20,16},{24,28},{28,24},{1,5},{5... | collective-permute-start | bytes 681992 | tf_op jit(solution)/shard_map/ppermute | solution.py:296
  11.8 8.6 %collective-permute-start.1 = (bf16[2,24,4736]{2,1,0:T(8,128)(2,1)S(1)}, bf16[2,24,4736]{2,1,0:T(8,128)(2,1)S(1)}, u32[]{:S(2)}, u32[]{:S(2)}) collective-permute-start(bf16[2,24,4736]{2,1,0:T(8,128)(2,1)S(1)} %pad_maximum_fusion.1), channel_id=1, source_target_pairs={{0,1},{1,0},{2,3},{3,2},{4,5},{5,4},{6,7},{7,6},{8,9},{9,8},{10,11... | collective-permute-start | bytes 1363976 | tf_op jit(solution)/shard_map/ppermute | solution.py:296
  11.9 8.0 %collective-permute-start.7 = (bf16[1,24,4736]{2,1,0:T(8,128)(2,1)S(1)}, bf16[1,24,4736]{2,1,0:T(8,128)(2,1)S(1)}, u32[]{:S(2)}, u32[]{:S(2)}) collective-permute-start(bf16[1,24,4736]{2,1,0:T(8,128)(2,1)S(1)} %collective-permute-done.5.refs_3_), channel_id=1, source_target_pairs={{0,8},{4,0},{8,16},{12,4},{16,24},{20,12},{24,28},{28,20},{1,9},{5... | collective-permute-start | bytes 681992 | tf_op jit(solution)/shard_map/ppermute | solution.py:307
  13.2 9.9 %collective-permute-start.6 = (bf16[1,24,4736]{2,1,0:T(8,128)(2,1)S(1)}, bf16[1,24,4736]{2,1,0:T(8,128)(2,1)S(1)}, u32[]{:S(2)}, u32[]{:S(2)}) collective-permute-start(bf16[1,24,4736]{2,1,0:T(8,128)(2,1)S(1)} %collective-permute-done.5.refs_3_), channel_id=1, source_target_pairs={{0,2},{1,3},{2,0},{3,1},{4,6},{5,7},{6,4},{7,5},{8,10},{9,11},{10,... | collective-permute-start | bytes 681992 | tf_op jit(solution)/shard_map/ppermute | solution.py:296
  19.9 7.0 %collective-permute-start.9 = (bf16[1,24,4736]{2,1,0:T(8,128)(2,1)S(1)}, bf16[1,24,4736]{2,1,0:T(8,128)(2,1)S(1)}, u32[]{:S(2)}, u32[]{:S(2)}) collective-permute-start(bf16[1,24,4736]{2,1,0:T(8,128)(2,1)S(1)} %collective-permute-done.7.refs_6_), channel_id=1, source_target_pairs={{0,2},{1,3},{2,0},{3,1},{4,6},{5,7},{6,4},{7,5},{8,10},{9,11},{10,... | collective-permute-start | bytes 681992 | tf_op jit(solution)/shard_map/ppermute | solution.py:296
  20.4 6.5 %collective-permute-start.2 = (bf16[4,24,128]{2,1,0:T(8,128)(2,1)S(1)}, bf16[4,24,128]{2,1,0:T(8,128)(2,1)S(1)}, u32[]{:S(2)}, u32[]{:S(2)}) collective-permute-start(bf16[4,24,128]{2,1,0:T(8,128)(2,1)S(1)} %pad_maximum_fusion.3), channel_id=1, source_target_pairs={{0,16},{4,20},{8,24},{12,28},{16,0},{20,4},{24,8},{28,12},{1,17},{... | collective-permute-start | bytes 73736 | tf_op jit(solution)/shard_map/ppermute | solution.py:296
  23.2 12.7 %collective-permute-start.8 = (bf16[3,24,4736]{2,1,0:T(8,128)(2,1)S(1)}, bf16[3,24,4736]{2,1,0:T(8,128)(2,1)S(1)}, u32[]{:S(2)}, u32[]{:S(2)}) collective-permute-start(bf16[3,24,4736]{2,1,0:T(8,128)(2,1)S(1)} %pad_maximum_fusion), channel_id=1, source_target_pairs={{0,1},{1,0},{2,3},{3,2},{4,5},{5,4},{6,7},{7,6},{8,9},{9,8},{10,11... | collective-permute-start | bytes 2045960 | tf_op jit(solution)/shard_map/ppermute | solution.py:296
  26.9 9.0 %collective-permute-start.10 = (bf16[1,24,4736]{2,1,0:T(8,128)(2,1)S(1)}, bf16[1,24,4736]{2,1,0:T(8,128)(2,1)S(1)}, u32[]{:S(2)}, u32[]{:S(2)}) collective-permute-start(bf16[1,24,4736]{2,1,0:T(8,128)(2,1)S(1)} %collective-permute-done.9.refs_7_), channel_id=1, source_target_pairs={{0,1},{1,0},{2,3},{3,2},{4,5},{5,4},{6,7},{7,6},{8,9},{9,8},{10,11... | collective-permute-start | bytes 681992 | tf_op jit(solution)/shard_map/ppermute | solution.py:296
  26.9 4.2 %collective-permute-start.3 = (bf16[8,24,128]{2,1,0:T(8,128)(2,1)S(1)}, bf16[8,24,128]{2,1,0:T(8,128)(2,1)S(1)}, u32[]{:S(2)}, u32[]{:S(2)}) collective-permute-start(bf16[8,24,128]{2,1,0:T(8,128)(2,1)S(1)} %pad_maximum_fusion.2), channel_id=1, source_target_pairs={{0,8},{4,12},{8,0},{12,4},{16,24},{20,28},{24,16},{28,20},{1,9},{5... | collective-permute-start | bytes 147464 | tf_op jit(solution)/shard_map/ppermute | solution.py:296
  31.2 4.7 %collective-permute-start.4 = (bf16[16,24,128]{2,1,0:T(8,128)(2,1)S(1)}, bf16[16,24,128]{2,1,0:T(8,128)(2,1)S(1)}, u32[]{:S(2)}, u32[]{:S(2)}) collective-permute-start(bf16[16,24,128]{2,1,0:T(8,128)(2,1)S(1)} %get-tuple-element.22), channel_id=1, source_target_pairs={{0,4},{4,0},{8,12},{12,8},{16,20},{20,16},{24,28},{28,24},{1,5},{5... | collective-permute-start | bytes 294920 | tf_op jit(solution)/shard_map/ppermute | solution.py:296
  35.9 52.6 %copy-start = (bf16[64,64,128]{2,1,0:T(8,128)(2,1)S(1)}, bf16[64,64,128]{2,1,0:T(8,128)(2,1)}, u32[]{:S(2)}) copy-start(bf16[64,64,128]{2,1,0:T(8,128)(2,1)} %param.11) | copy-start | bytes 3145732
  35.9 52.6 %copy-start.1 = (bf16[8,64,512]{2,1,0:T(8,128)(2,1)S(1)}, bf16[8,64,512]{2,1,0:T(8,128)(2,1)}, u32[]{:S(2)}) copy-start(bf16[8,64,512]{2,1,0:T(8,128)(2,1)} %param.12) | copy-start | bytes 1572868
  35.9 52.6 %copy-start.3 = (bf16[1,64,512]{2,1,0:T(8,128)(2,1)S(1)}, bf16[1,64,512]{2,1,0:T(8,128)(2,1)}, u32[]{:S(2)}) copy-start(bf16[1,64,512]{2,1,0:T(8,128)(2,1)} %param.13) | copy-start | bytes 196612
